TPU v7x, 32 devices: a whole 2x2x4 slice. The times are simulated.
32 devices in a mesh: rows: 4 (over x, core), labels: 8 (over z, y).
Axes of the slice: x: 2, y: 2, z: 4, core: 2. Of those that a mesh axis runs over, the one named last changes fastest.
Arguments:
- pool_features: bfloat16 [512, 768], P('rows'), may hold values from -6 to 6
- pool_labels: int32 [512, 16], P('rows'), may hold values from 0 to 12287
- pool_counts: int32 [512], P('rows'), may hold values from 1 to 16
- batch_rows: int32 [2, 128], P(None, 'rows'), may hold values from 0 to 127
- weights: float32 [12288, 768], P(('rows', 'labels')), may hold values from -0.21875 to 0.21875
- momentum: float32 [12288, 768], P(('rows', 'labels')), may hold values from -24 to 24
Outputs:
- new_weights: float32 [12288, 768], P(('rows', 'labels'))
- new_momentum: float32 [12288, 768], P(('rows', 'labels'))
- feature_grads: float32 [2, 128, 768], P(None, 'rows')
Inputs may be any that keep to these rules, and one draw needn't show every extreme that they name: `pool_labels`: slots of a list at or past its count are padding and are ignored; a label may appear twice in a list. `batch_rows`: an entry names one of the 128 examples stored with the index of rows that owns that batch row.
All inputs are finite; a program needn't handle non-finite values.
Results may differ from a plain program's by a relative error of at most 0.00045.
The roundings to bfloat16 on the way count: a program that leaves them out, or rounds other values in their place, can miss the bound.
Values may be sent and summed in bfloat16 or wider, within the bound.
No kernel may reach another device: no remote copies, remote signals or barrier semaphores. Data moves between devices by JAX's collectives and lax.ppermute only.
A program may use at most 64 MiB of HBM per device.

v0:
```python
import jax
import jax.numpy as jnp
from jax import lax
from jax.sharding import PartitionSpec as P

learn_rate = 0.001
decay_rate = 0.9


def feature_sums(errors_list, lowered_list, width):
    parts = []
    for errors, low_weights in zip(errors_list, lowered_list):
        parts.append(jnp.dot(errors, low_weights, preferred_element_type=jnp.float32))
    grouped = lax.psum_scatter(
        jnp.concatenate(parts, axis=1), "rows", scatter_dimension=0, tiled=True
    )
    mine = lax.psum(grouped, "labels")
    return jnp.stack([mine[:, :width], mine[:, width:]])


def per_device(pool_features, pool_labels, pool_counts, batch_rows, weights, momentum):
    lab_rows = weights.shape[0]
    width = weights.shape[1]
    device_index = lax.axis_index("rows") * lax.axis_size("labels") + lax.axis_index("labels")
    labels = device_index * lab_rows + jnp.arange(lab_rows, dtype=jnp.int32)
    all_ids, all_counts = (
        lax.all_gather(pool_labels[batch_rows], "rows", axis=1, tiled=True),
        lax.all_gather(pool_counts[batch_rows], "rows", axis=1, tiled=True),
    )
    all_features = lax.all_gather(pool_features[batch_rows], "rows", axis=1, tiled=True)
    errors_list = []
    lowered_list = []
    for batch in range(2):
        features = all_features[batch]
        label_ids = all_ids[batch]
        in_list = (
            jnp.arange(label_ids.shape[1], dtype=jnp.int32)[None, :] < all_counts[batch][:, None]
        )
        matched = (label_ids[:, :, None] == labels[None, None, :]) & in_list[:, :, None]
        targets = jnp.any(matched, axis=1).astype(jnp.float32)
        low_weights = weights.astype(jnp.bfloat16)
        logits = lax.dot_general(
            features, low_weights, (((1,), (1,)), ((), ())), preferred_element_type=jnp.float32
        )
        errors = (jax.nn.sigmoid(logits) - targets).astype(jnp.bfloat16)
        grads = lax.dot_general(
            errors, features, (((0,), (0,)), ((), ())), preferred_element_type=jnp.float32
        )
        errors_list.append(errors)
        lowered_list.append(low_weights)
        momentum = decay_rate * momentum + grads
        weights = weights - learn_rate * momentum
    return (weights, momentum, feature_sums(errors_list, lowered_list, width))


def solution(mesh):
    in_specs = (
        P("rows", None),
        P("rows", None),
        P("rows"),
        P(None, "rows"),
        P(("rows", "labels"), None),
        P(("rows", "labels"), None),
    )
    out_specs = (P(("rows", "labels"), None), P(("rows", "labels"), None), P(None, "rows", None))
    return jax.shard_map(
        per_device, mesh=mesh, in_specs=in_specs, out_specs=out_specs, check_vma=False
    )
```

profile of v0, /device:TPU:0, one launch (start us, length us, event | category | flops | bytes accessed | tf_op | source)
XLA Modules:
  0.0 143.2 jit_solution(4166280901989840444)
XLA Ops:
  7.2 0.0 copy-start
  7.2 0.0 reduce-scatter.2.cloned.1.call-start
  7.2 0.7 compare_select_fusion
  7.9 0.1 reshape.62
  8.0 1.4 gather_fusion.2
  9.5 0.1 reshape.81
  9.6 6.0 %all-gather.3 = s32[4,32,2]{1,2,0:T(2,128)S(1)} all-gather(s32[1,32,2]{1,2,0:T(2,128)S(1)} %bitcast.41), channel_id=4, replica_groups=mesh['rows'=4,'labels'=8] {'rows'}, dimensions={0}, use_global_device_ids=true | all-gather | bytes 1280 | tf_op jit(solution)/shard_map/all_gather | solution.py:28
  15.6 0.1 reshape.94
  15.7 0.8 copy.14
  16.5 0.0 copy-start.1
  16.5 0.6 gather_fusion.1
  17.1 0.0 copy-done
  17.1 0.7 gather_fusion
  17.8 5.7 %all-gather.1 = s32[2,128,16]{2,1,0:T(8,128)S(1)} all-gather(s32[2,32,16]{2,1,0:T(8,128)S(1)} %bitcast.39), channel_id=3, replica_groups=mesh['rows'=4,'labels'=8] {'rows'}, dimensions={1}, use_global_device_ids=true | all-gather | bytes 20480 | tf_op jit(solution)/shard_map/all_gather | solution.py:27
  23.5 6.7 %all-gather = bf16[2,128,768]{2,1,0:T(8,128)(2,1)S(1)} all-gather(bf16[2,32,768]{2,1,0:T(8,128)(2,1)S(1)} %bitcast.38), channel_id=2, replica_groups=mesh['rows'=4,'labels'=8] {'rows'}, dimensions={1}, use_global_device_ids=true | all-gather | bytes 491520 | tf_op jit(solution)/shard_map/all_gather | solution.py:30
  30.2 0.1 iota_compare_fusion
  30.3 2.0 %and_reduce_fusion = (pred[128,384]{1,0:T(8,128)(4,1)S(1)}, pred[128,384]{1,0:T(8,128)(4,1)S(1)}) fusion(s32[128,16]{1,0:T(8,128)S(1)} %get-tuple-element.8, s32[384]{0:T(512)S(1)} %iota_add_fusion, pred[128,16]{1,0:T(8,128)(4,1)S(1)} %get-tuple-element.15, pred[128,16]{1,0:T(8,128)(4,1)S(1)} %get-tuple-element.16, s32[128,16]{1,0:T(8,128)S(1)} %get-tuple-element.7), kind=kLoop, calls=%fused_computation.3 | loop fusion | flops 4620288 | bytes 120320 | tf_op jit(solution)/shard_map/reduce_or | solution.py:40
  32.4 0.0 copy-done.1
  32.4 0.3 fusion.9
  32.7 0.0 copy-start.2
  32.7 0.3 fusion.11
  33.0 1.0 copy-done.2
  34.0 0.4 fusion.10
  34.4 0.3 fusion.8
  34.7 0.3 fusion.14
  35.0 1.0 pad_maximum_fusion
  36.0 0.0 reduce-scatter.2.cloned.1.call-update
  36.0 0.0 all-reduce.2.cloned.1.call-start
  36.0 24.7 %reduce-scatter.2.cloned.1.call-done = f32[32,1536]{1,0:T(8,128)} async-done(((f32[128,1536]{1,0:T(8,128)}), f32[32,1536]{1,0:T(8,128)}) %reduce-scatter.2.cloned.1.call-update) | async-done | bytes 196624 | tf_op jit(solution)/shard_map/reduce_scatter | solution.py:14
  60.7 0.0 all-reduce.2.cloned.1.call-update
  60.7 1.9 %multiply_subtract_fusion = (f32[384,768]{1,0:T(8,128)}, f32[384,768]{1,0:T(8,128)}) fusion(f32[384,768]{1,0:T(8,128)S(1)} %copy-done.1, f32[384,768]{1,0:T(8,128)S(1)} %get-tuple-element.12, bf16[128,384]{1,0:T(8,128)(2,1)S(1)} %fusion.8, bf16[2,128,768]{2,1,0:T(8,128)(2,1)S(1)} %all-gather), kind=kOutput, calls=%fused_computation.7 | convolution fusion | flops 77266944 | bytes 5013504 | tf_op jit(solution)/shard_map/dot_general | solution.py:46
  62.6 72.1 %all-reduce.2.cloned.1.call-done = f32[32,1536]{1,0:T(8,128)} async-done(((f32[32,1536]{1,0:T(8,128)}), f32[32,1536]{1,0:T(8,128)}) %all-reduce.2.cloned.1.call-update) | async-done | bytes 196624 | tf_op jit(solution)/shard_map/psum | solution.py:17
  134.7 1.0 slice_bitcast_fusion.7
  135.6 0.7 pad_maximum_fusion.1
  (5 shorter events, 0.0 us)
Async XLA Ops:
  7.2 9.9 %copy-start = (bf16[128,768]{1,0:T(8,128)(2,1)S(1)}, bf16[128,768]{1,0:T(8,128)(2,1)}, u32[]{:S(2)}) copy-start(bf16[128,768]{1,0:T(8,128)(2,1)} %param.6) | copy-start | bytes 589828
  7.2 53.5 %reduce-scatter.2.cloned.1.call-start = ((), (), s32[]{:S(2)}) async-start(), calls=%async_computation.1 | async-start | bytes 983040 | tf_op jit(solution)/shard_map/reduce_scatter | solution.py:14
  16.5 15.9 %copy-start.1 = (f32[384,768]{1,0:T(8,128)S(1)}, f32[384,768]{1,0:T(8,128)}, u32[]{:S(2)}) copy-start(f32[384,768]{1,0:T(8,128)} %param.10) | copy-start | bytes 3538948
  32.7 1.3 copy-start.2
  36.0 98.7 %all-reduce.2.cloned.1.call-start = ((), (), s32[]{:S(2)}) async-start(), calls=%async_computation.2 | async-start | bytes 393216 | tf_op jit(solution)/shard_map/psum | solution.py:17
Sparse Core Ops, SparseCore 0:
  36.1 24.5 reduce-scatter.1
  64.0 70.6 all-reduce.1
where the time goes:
time: 143 us
  waiting for transfers between devices  96.8 us (68%)
  blocking collectives  18.4 us (13%)
  between operations  14.1 us (10%)
  local copies, waits for them, and re-layouts  5.77 us (4%)
  other arithmetic  4.51 us (3%)
  matrix products  3.49 us (2%)
    psum x1, waiting for transfers between devices, feature_sums(): mine = lax.psum(grouped, 'labels')  72.1 us
    reduce_scatter x1, waiting for transfers between devices, feature_sums(): lax.psum_scatter(jnp.concatenate(parts, axis=1), 'rows', scatter_dimensio...  24.7 us
    all_gather x1, blocking collectives, per_device(): lax.all_gather(pool_features[batch_rows], 'rows', axis=1, tiled=True)  6.67 us
    all_gather x1, blocking collectives, per_device(): lax.all_gather(pool_counts[batch_rows], 'rows', axis=1, tiled=True)  6.01 us
    all_gather x1, blocking collectives, per_device(): lax.all_gather(pool_labels[batch_rows], 'rows', axis=1, tiled=True)  5.73 us
  transfers between devices with their start and end apart: 2, of which 2 were waited for; matrix products, arithmetic and copies ran while one was open for 1% of the time, Pallas kernels for 0%

commit v1 on v0

--- a/solution.py
+++ b/solution.py
@@ -14,7 +14,8 @@
     grouped = lax.psum_scatter(
         jnp.concatenate(parts, axis=1), "rows", scatter_dimension=0, tiled=True
     )
-    mine = lax.psum(grouped, "labels")
+    pieces = lax.all_gather(grouped, "labels", axis=0, tiled=False)
+    mine = pieces.sum(axis=0)
     return jnp.stack([mine[:, :width], mine[:, width:]])
 
 

time: 143 us -> 116 us (0.81)
  waiting for transfers between devices: 96.8 us -> 69.2 us
  other arithmetic: 4.51 us -> 6.02 us
    psum x1 -> x0, waiting for transfers between devices: 72.1 us -> none  [feature_sums(): mine = lax.psum(grouped, 'labels')]
    all_gather x0 -> x1, waiting for transfers between devices: none -> 44.5 us  [feature_sums(): pieces = lax.all_gather(grouped, 'labels', axis=0, tiled=False)]
    reduce_sum x0 -> x1, other arithmetic: none -> 1.51 us  [feature_sums(): mine = pieces.sum(axis=0)]
  transfers between devices with their start and end apart: 2 -> 2, of which waited for: 2 -> 2; matrix products, arithmetic and copies ran while one was open for 1% -> 2% of each run, Pallas kernels for 0% -> 0%
where the time goes in v1:
time: 116 us
  waiting for transfers between devices  69.2 us (60%)
  blocking collectives  18.4 us (16%)
  between operations  14.1 us (12%)
  other arithmetic  6.02 us (5%)
  local copies, waits for them, and re-layouts  4.83 us (4%)
  matrix products  3.49 us (3%)
    all_gather x1, waiting for transfers between devices, feature_sums(): pieces = lax.all_gather(grouped, 'labels', axis=0, tiled=False)  44.5 us
    reduce_scatter x1, waiting for transfers between devices, feature_sums(): lax.psum_scatter(jnp.concatenate(parts, axis=1), 'rows', scatter_dimensio...  24.7 us
    all_gather x1, blocking collectives, per_device(): lax.all_gather(pool_features[batch_rows], 'rows', axis=1, tiled=True)  6.67 us
    all_gather x1, blocking collectives, per_device(): lax.all_gather(pool_counts[batch_rows], 'rows', axis=1, tiled=True)  6.01 us
    all_gather x1, blocking collectives, per_device(): lax.all_gather(pool_labels[batch_rows], 'rows', axis=1, tiled=True)  5.73 us
  transfers between devices with their start and end apart: 2, of which 2 were waited for; matrix products, arithmetic and copies ran while one was open for 2% of the time, Pallas kernels for 0%

profile of v1, /device:TPU:0, one launch (start us, length us, event | category | flops | bytes accessed | tf_op | source)
XLA Modules:
  0.0 116.2 jit_solution(13316181050092365854)
XLA Ops:
  7.2 0.0 copy-start
  7.2 0.0 reduce-scatter.2.cloned.1.call-start
  7.2 0.7 compare_select_fusion
  7.9 0.1 reshape.62
  8.0 1.4 %gather_fusion.2 = s32[64]{0:T(128)S(1)} fusion(s32[128]{0:T(128)} %param.8, s32[1024]{0:T(1024)S(1)} %pad_clamp_fusion), kind=kCustom, calls=%fused_computation.2 | custom fusion | bytes 768 | tf_op jit(solution)/shard_map/gather | solution.py:29
  9.5 0.1 reshape.81
  9.6 6.0 %all-gather.4 = s32[4,32,2]{1,2,0:T(2,128)S(1)} all-gather(s32[1,32,2]{1,2,0:T(2,128)S(1)} %bitcast.43), channel_id=4, replica_groups=mesh['rows'=4,'labels'=8] {'rows'}, dimensions={0}, use_global_device_ids=true | all-gather | bytes 1280 | tf_op jit(solution)/shard_map/all_gather | solution.py:29
  15.6 0.1 reshape.95
  15.7 0.8 copy.14
  16.5 0.0 copy-start.1
  16.5 0.6 gather_fusion.1
  17.1 0.0 copy-done
  17.1 0.7 gather_fusion
  17.8 5.7 %all-gather.1 = s32[2,128,16]{2,1,0:T(8,128)S(1)} all-gather(s32[2,32,16]{2,1,0:T(8,128)S(1)} %bitcast.41), channel_id=3, replica_groups=mesh['rows'=4,'labels'=8] {'rows'}, dimensions={1}, use_global_device_ids=true | all-gather | bytes 20480 | tf_op jit(solution)/shard_map/all_gather | solution.py:28
  23.5 6.7 %all-gather = bf16[2,128,768]{2,1,0:T(8,128)(2,1)S(1)} all-gather(bf16[2,32,768]{2,1,0:T(8,128)(2,1)S(1)} %bitcast.40), channel_id=2, replica_groups=mesh['rows'=4,'labels'=8] {'rows'}, dimensions={1}, use_global_device_ids=true | all-gather | bytes 491520 | tf_op jit(solution)/shard_map/all_gather | solution.py:31
  30.2 0.1 iota_compare_fusion
  30.3 2.0 %and_reduce_fusion = (pred[128,384]{1,0:T(8,128)(4,1)S(1)}, pred[128,384]{1,0:T(8,128)(4,1)S(1)}) fusion(s32[128,16]{1,0:T(8,128)S(1)} %get-tuple-element.8, s32[384]{0:T(512)S(1)} %iota_add_fusion, pred[128,16]{1,0:T(8,128)(4,1)S(1)} %get-tuple-element.15, pred[128,16]{1,0:T(8,128)(4,1)S(1)} %get-tuple-element.16, s32[128,16]{1,0:T(8,128)S(1)} %get-tuple-element.7), kind=kLoop, calls=%fused_computation.3 | loop fusion | flops 4620288 | bytes 120320 | tf_op jit(solution)/shard_map/reduce_or | solution.py:41
  32.4 0.0 copy-done.1
  32.4 0.3 fusion.9
  32.7 0.0 copy-start.2
  32.7 0.3 fusion.11
  33.0 1.0 copy-done.2
  34.0 0.4 fusion.10
  34.4 0.3 fusion.8
  34.7 0.3 fusion.14
  35.0 1.0 pad_maximum_fusion
  36.0 0.0 reduce-scatter.2.cloned.1.call-update
  36.0 0.0 all-gather.7.cloned.1.call-start
  36.0 24.7 %reduce-scatter.2.cloned.1.call-done = f32[32,1536]{1,0:T(8,128)} async-done(((f32[128,1536]{1,0:T(8,128)}), f32[32,1536]{1,0:T(8,128)}) %reduce-scatter.2.cloned.1.call-update) | async-done | bytes 196624 | tf_op jit(solution)/shard_map/reduce_scatter | solution.py:14
  60.7 0.0 all-gather.7.cloned.1.call-update
  60.7 1.9 %multiply_subtract_fusion = (f32[384,768]{1,0:T(8,128)}, f32[384,768]{1,0:T(8,128)}) fusion(f32[384,768]{1,0:T(8,128)S(1)} %copy-done.1, f32[384,768]{1,0:T(8,128)S(1)} %get-tuple-element.12, bf16[128,384]{1,0:T(8,128)(2,1)S(1)} %fusion.8, bf16[2,128,768]{2,1,0:T(8,128)(2,1)S(1)} %all-gather), kind=kOutput, calls=%fused_computation.7 | convolution fusion | flops 77266944 | bytes 5013504 | tf_op jit(solution)/shard_map/dot_general | solution.py:47
  62.6 44.5 %all-gather.7.cloned.1.call-done = f32[256,1536]{1,0:T(8,128)} async-done(((f32[32,1536]{1,0:T(8,128)}), f32[256,1536]{1,0:T(8,128)}) %all-gather.7.cloned.1.call-update) | async-done | bytes 1572880 | tf_op jit(solution)/shard_map/all_gather | solution.py:17
  107.1 1.5 %reduce_sum.9 = f32[32,1536]{1,0:T(8,128)S(1)} reduce(f32[8,32,1536]{2,1,0:T(8,128)} %bitcast.39, f32[]{:T(128)} %constant.25.clone.1), dimensions={0}, to_apply=%region_3.0 | reduce | flops 344064 | bytes 1769476 | tf_op jit(solution)/shard_map/reduce_sum | solution.py:18
  108.6 0.7 pad_maximum_fusion.1
  (6 shorter events, 0.0 us)
Async XLA Ops:
  7.2 9.9 %copy-start = (bf16[128,768]{1,0:T(8,128)(2,1)S(1)}, bf16[128,768]{1,0:T(8,128)(2,1)}, u32[]{:S(2)}) copy-start(bf16[128,768]{1,0:T(8,128)(2,1)} %param.6) | copy-start | bytes 589828
  7.2 53.5 %reduce-scatter.2.cloned.1.call-start = ((), (), s32[]{:S(2)}) async-start(), calls=%async_computation.1 | async-start | bytes 983040 | tf_op jit(solution)/shard_map/reduce_scatter | solution.py:14
  16.5 15.9 %copy-start.1 = (f32[384,768]{1,0:T(8,128)S(1)}, f32[384,768]{1,0:T(8,128)}, u32[]{:S(2)}) copy-start(f32[384,768]{1,0:T(8,128)} %param.10) | copy-start | bytes 3538948
  32.7 1.3 %copy-start.2 = (f32[384,768]{1,0:T(8,128)S(1)}, f32[384,768]{1,0:T(8,128)}, u32[]{:S(2)}) copy-start(f32[384,768]{1,0:T(8,128)} %param.11) | copy-start | bytes 3538948
  36.0 71.1 %all-gather.7.cloned.1.call-start = ((), (), s32[]{:S(2)}) async-start(), calls=%async_computation.2 | async-start | bytes 1769472 | tf_op jit(solution)/shard_map/all_gather | solution.py:17
Sparse Core Ops, SparseCore 0:
  36.1 24.5 reduce-scatter.1
  62.9 44.1 all-gather.6
